TPU v7x, 32 devices: a whole 2x2x4 slice. The times are simulated.
32 devices in a mesh: segment: 2 (over x), expert: 16 (over z, y, core).
Axes of the slice: x: 2, y: 2, z: 4, core: 2. Of those that a mesh axis runs over, the one named last changes fastest.
Arguments:
- fwd_acts: bfloat16 [2, 384, 2048], P('segment', 'expert'), may hold values from -6 to 6
- fwd_ids: int32 [2, 384, 8], P('segment', 'expert'), may hold values from 0 to 15, all different within a row; in each aligned block of 24 rows (0 to 23, 24 to 47, ..., all dimensions but the last counted through in order) at most 12 rows name the same one
- fwd_prob: float32 [2, 384, 8], P('segment', 'expert'), may hold values from 0.02 to 0.3
- bwd_acts: bfloat16 [2, 384, 2048], P('segment', 'expert'), may hold values from -6 to 6
- bwd_ids: int32 [2, 384, 8], P('segment', 'expert'), may hold values from 0 to 15, all different within a row; in each aligned block of 24 rows (0 to 23, 24 to 47, ..., all dimensions but the last counted through in order) at most 12 rows name the same one
- bwd_prob: float32 [2, 384, 8], P('segment', 'expert'), may hold values from 0.02 to 0.3
- grad_in: bfloat16 [2, 384, 2048], P('segment', 'expert'), may hold values from -6 to 6
- w_gate: bfloat16 [2, 16, 2048, 384], P('segment', 'expert'), may hold values from -0.125 to 0.125
- w_up: bfloat16 [2, 16, 2048, 384], P('segment', 'expert'), may hold values from -0.125 to 0.125
- w_down: bfloat16 [2, 16, 384, 2048], P('segment', 'expert'), may hold values from -0.3125 to 0.3125
Outputs:
- fwd_out: bfloat16 [2, 384, 2048], P('segment', 'expert')
- bwd_out: bfloat16 [2, 384, 2048], P('segment', 'expert')
Inputs may be any that keep to these rules, and one draw needn't show every extreme that they name: `fwd_ids`: each token names 8 different experts. Among the 24 tokens of one block no expert is named by more than 12 tokens, and in every draw some expert is named by exactly 12 tokens of a block. `bwd_ids`: as for fwd_ids.
All inputs are finite; a program needn't handle non-finite values.
Results may differ from a plain program's by a relative error of at most 0.0064.
Values may be sent and summed in bfloat16 or wider, within the bound.
A program may use at most 64 MiB of HBM per device.

v0:
```python
import jax
import jax.numpy as jnp
from jax import lax
from jax.sharding import PartitionSpec as P

TOP = 8


def shifted(array, axis, by):
    count = lax.axis_size(axis)
    return lax.ppermute(array, axis, [(i, (i + by) % count) for i in range(count)])


def routing(expert_ids, gate_prob, experts, capacity):
    tok_count = expert_ids.shape[0]
    pick_count = expert_ids.shape[1]
    entry_count = tok_count * pick_count
    flat_ids = expert_ids.reshape(entry_count)
    one_hot = (flat_ids[:, None] == jnp.arange(experts, dtype=jnp.int32)[None, :]).astype(
        jnp.float32
    )
    entry_index = jnp.arange(entry_count, dtype=jnp.int32)
    strictly_lower = (entry_index[:, None] > entry_index[None, :]).astype(jnp.float32)
    earlier = jnp.dot(strictly_lower, one_hot, precision=lax.Precision.HIGHEST)
    slot_index = jnp.sum(earlier * one_hot, axis=1)
    slot_range = jnp.arange(capacity, dtype=jnp.int32).astype(jnp.float32)
    slot_hot = (slot_range[None, :] == slot_index[:, None]).astype(jnp.float32)
    placed = (one_hot[:, :, None] * slot_hot[:, None, :]).reshape(
        tok_count, pick_count, experts * capacity
    )
    select_mat = jnp.sum(placed, axis=1)
    weigh_mat = jnp.sum(placed * gate_prob[:, :, None], axis=1)
    return (select_mat, weigh_mat)


def dispatch(select_mat, values):
    moved = lax.dot_general(
        select_mat.astype(jnp.bfloat16),
        values,
        (((0,), (0,)), ((), ())),
        preferred_element_type=jnp.float32,
    )
    return moved.astype(jnp.bfloat16)


def weigh_rows(weigh_mat, grads):
    moved = lax.dot_general(
        weigh_mat,
        grads.astype(jnp.float32),
        (((0,), (0,)), ((), ())),
        precision=lax.Precision.HIGHEST,
        preferred_element_type=jnp.float32,
    )
    return moved.astype(jnp.bfloat16)


def collect(matrix, rows):
    return jnp.dot(matrix, rows.astype(jnp.float32), precision=lax.Precision.HIGHEST).astype(
        jnp.bfloat16
    )


def expert_forward(rows, gate_mat, up_mat, down_mat):
    gate_pre = jnp.dot(rows, gate_mat, preferred_element_type=jnp.float32)
    up_pre = jnp.dot(rows, up_mat, preferred_element_type=jnp.float32)
    hidden = (jax.nn.silu(gate_pre) * up_pre).astype(jnp.bfloat16)
    return jnp.dot(hidden, down_mat, preferred_element_type=jnp.float32).astype(jnp.bfloat16)


def expert_backward(rows, grad_rows, gate_mat, up_mat, down_mat):
    contract = (((1,), (1,)), ((), ()))
    gate_pre = jnp.dot(rows, gate_mat, preferred_element_type=jnp.float32)
    up_pre = jnp.dot(rows, up_mat, preferred_element_type=jnp.float32)
    grad_hidden = lax.dot_general(grad_rows, down_mat, contract, preferred_element_type=jnp.float32)
    sigma = jax.nn.sigmoid(gate_pre)
    grad_gate = (grad_hidden * up_pre * sigma * (1.0 + gate_pre * (1.0 - sigma))).astype(
        jnp.bfloat16
    )
    grad_up = (grad_hidden * gate_pre * sigma).astype(jnp.bfloat16)
    back = lax.dot_general(grad_gate, gate_mat, contract, preferred_element_type=jnp.float32)
    back = back + lax.dot_general(grad_up, up_mat, contract, preferred_element_type=jnp.float32)
    return back.astype(jnp.bfloat16)


def body(fwd_acts, fwd_ids, fwd_prob, bwd_acts, bwd_ids, bwd_prob, grad_in, w_gate, w_up, w_down):
    experts = lax.axis_size("expert")
    tok_count = fwd_acts.shape[1]
    width = fwd_acts.shape[2]
    capacity = max(2, (tok_count * TOP + experts - 1) // experts)
    gate_mat = w_gate[0, 0]
    up_mat = w_up[0, 0]
    down_mat = w_down[0, 0]
    fwd_select, fwd_weigh = routing(fwd_ids[0], fwd_prob[0], experts, capacity)
    bwd_select, bwd_weigh = routing(bwd_ids[0], bwd_prob[0], experts, capacity)
    fwd_rows = dispatch(fwd_select, fwd_acts[0]).reshape(experts, capacity, width)
    bwd_rows = dispatch(bwd_select, bwd_acts[0]).reshape(experts, capacity, width)
    grad_rows = weigh_rows(bwd_weigh, grad_in[0]).reshape(experts, capacity, width)

    def backward_rows(received, received_grad):
        flat_grad = received_grad.reshape(-1, width)
        return expert_backward(
            received.reshape(-1, width), flat_grad, gate_mat, up_mat, down_mat
        ).reshape(received.shape)

    received = lax.all_to_all(fwd_rows, "expert", split_axis=0, concat_axis=0, tiled=True)
    fwd_back = lax.all_to_all(
        expert_forward(received.reshape(-1, width), gate_mat, up_mat, down_mat).reshape(
            received.shape
        ),
        "expert",
        split_axis=0,
        concat_axis=0,
        tiled=True,
    )
    received = (
        lax.all_to_all(bwd_rows, "expert", split_axis=0, concat_axis=0, tiled=True),
        lax.all_to_all(grad_rows, "expert", split_axis=0, concat_axis=0, tiled=True),
    )
    bwd_back = lax.all_to_all(
        backward_rows(received[0], received[1]), "expert", split_axis=0, concat_axis=0, tiled=True
    )
    fwd_result = collect(fwd_weigh, fwd_back.reshape(-1, width))
    bwd_result = collect(bwd_select, bwd_back.reshape(-1, width))
    fwd_out = shifted(fwd_result[None], "segment", 1)
    bwd_out = shifted(bwd_result[None], "segment", -1)
    return (fwd_out, bwd_out)


def solution(mesh):
    return jax.shard_map(
        body,
        mesh=mesh,
        in_specs=(
            P("segment", "expert", None),
            P("segment", "expert", None),
            P("segment", "expert", None),
            P("segment", "expert", None),
            P("segment", "expert", None),
            P("segment", "expert", None),
            P("segment", "expert", None),
            P("segment", "expert", None, None),
            P("segment", "expert", None, None),
            P("segment", "expert", None, None),
        ),
        out_specs=(P("segment", "expert", None), P("segment", "expert", None)),
        check_vma=False,
    )
```

profile of v0, /device:TPU:0, one launch (start us, length us, event | category | flops | bytes accessed | tf_op | source)
XLA Modules:
  0.0 170.6 jit_solution(9495040957352861436)
XLA Ops:
  0.6 0.0 copy-start
  0.7 0.9 copy.26
  1.5 0.1 eq.79
  1.6 0.2 fusion.40
  1.8 0.8 copy.22
  2.6 0.1 eq.72
  2.7 0.2 fusion.39
  2.9 1.4 copy.25
  4.2 1.4 copy.29
  5.6 0.1 compare_convert_fusion
  5.6 0.1 copy.28
  5.8 0.1 copy.23
  5.9 0.1 copy.27
  6.0 0.1 copy.24
  6.1 0.5 broadcast_multiply_fusion.1
  6.5 0.8 mul.89
  7.3 0.5 broadcast_multiply_fusion
  7.8 0.8 mul.99
  8.5 1.6 multiply_reduce_fusion
  10.1 1.7 %convolution_convert_fusion.1 = bf16[192,2048]{1,0:T(8,128)(2,1)S(1)} fusion(f32[24,192]{1,0:T(8,128)S(1)} %get-tuple-element.2, bf16[1,24,2048]{2,1,0:T(8,128)(2,1)} %param.16), kind=kOutput, calls=%fused_computation.3 | convolution fusion | flops 113639424 | bytes 903168 | tf_op jit(solution)/shard_map/dot_general | solution.py:47
  11.8 0.0 copy-start.5
  11.8 1.1 reshape.150
  13.0 7.4 %all-to-all-start.2 = ((bf16[16,12,2048]{2,1,0:T(8,128)(2,1)}), bf16[16,12,2048]{2,1,0:T(8,128)(2,1)S(1)}, u32[]{:S(2)}, u32[]{:S(2)}) async-start(bf16[16,12,2048]{2,1,0:T(8,128)(2,1)} %reshape.150), calls=%async_computation.2 | async-start | bytes 2097152 | tf_op jit(solution)/shard_map/all_to_all | solution.py:117
  20.4 0.0 copy-done.5
  20.4 0.4 convolution_convert_fusion.2
  20.8 0.0 copy-start.4
  20.8 1.2 reshape.146
  22.0 21.3 %all-to-all-done.2 = bf16[16,12,2048]{2,1,0:T(8,128)(2,1)S(1)} async-done(((bf16[16,12,2048]{2,1,0:T(8,128)(2,1)}), bf16[16,12,2048]{2,1,0:T(8,128)(2,1)S(1)}, u32[]{:S(2)}, u32[]{:S(2)}) %all-to-all-start.2) | async-done | bytes 786464 | tf_op jit(solution)/shard_map/all_to_all | solution.py:117
  43.3 6.8 %all-to-all-start = ((bf16[16,12,2048]{2,1,0:T(8,128)(2,1)}), bf16[16,12,2048]{2,1,0:T(8,128)(2,1)}, u32[]{:S(2)}, u32[]{:S(2)}) async-start(bf16[16,12,2048]{2,1,0:T(8,128)(2,1)} %reshape.146), calls=%async_computation | async-start | bytes 2097152 | tf_op jit(solution)/shard_map/all_to_all | solution.py:105
  50.1 0.0 copy-done.4
  50.2 1.3 convolution_convert_fusion
  51.4 0.0 copy-done.3
  51.5 1.2 reshape.152
  52.6 20.5 %all-to-all-done = bf16[16,12,2048]{2,1,0:T(8,128)(2,1)} async-done(((bf16[16,12,2048]{2,1,0:T(8,128)(2,1)}), bf16[16,12,2048]{2,1,0:T(8,128)(2,1)}, u32[]{:S(2)}, u32[]{:S(2)}) %all-to-all-start) | async-done | bytes 786464 | tf_op jit(solution)/shard_map/all_to_all | solution.py:105
  73.1 6.8 %all-to-all-start.3 = ((bf16[16,12,2048]{2,1,0:T(8,128)(2,1)}), bf16[16,12,2048]{2,1,0:T(8,128)(2,1)}, u32[]{:S(2)}, u32[]{:S(2)}) async-start(bf16[16,12,2048]{2,1,0:T(8,128)(2,1)} %reshape.152), calls=%async_computation.3 | async-start | bytes 2097152 | tf_op jit(solution)/shard_map/all_to_all | solution.py:116
  79.9 2.1 %reshape.147 = bf16[192,2048]{1,0:T(8,128)(2,1)} reshape(bf16[16,12,2048]{2,1,0:T(8,128)(2,1)} %all-to-all-done) | data formatting | bytes 1572864 | tf_op jit(solution)/shard_map/reshape | solution.py:107
  82.0 0.0 copy-done.1
  82.0 1.7 fusion.15
  83.7 0.0 copy-done
  83.7 3.6 %convolution_convert_fusion.3 = bf16[192,2048]{1,0:T(8,128)(2,1)} fusion(bf16[1,1,384,2048]{3,2,1,0:T(8,128)(2,1)} %param.19, bf16[192,2048]{1,0:T(8,128)(2,1)} %reshape.147, bf16[1,1,2048,384]{3,2,1,0:T(8,128)(2,1)S(1)} %copy-done, f32[192,384]{1,0:T(8,128)S(1)} %fusion.15), kind=kOutput, calls=%fused_computation.5 | convolution fusion | flops 604815360 | bytes 5013504 | tf_op jit(solution)/shard_map/dot_general | solution.py:67
  87.4 2.1 %reshape.148 = bf16[16,12,2048]{2,1,0:T(8,128)(2,1)} reshape(bf16[192,2048]{1,0:T(8,128)(2,1)} %convolution_convert_fusion.3) | data formatting | bytes 1572864 | tf_op jit(solution)/shard_map/reshape | solution.py:107
  89.5 13.4 %all-to-all-done.3 = bf16[16,12,2048]{2,1,0:T(8,128)(2,1)} async-done(((bf16[16,12,2048]{2,1,0:T(8,128)(2,1)}), bf16[16,12,2048]{2,1,0:T(8,128)(2,1)}, u32[]{:S(2)}, u32[]{:S(2)}) %all-to-all-start.3) | async-done | bytes 786464 | tf_op jit(solution)/shard_map/all_to_all | solution.py:116
  102.9 6.8 %all-to-all-start.1 = ((bf16[16,12,2048]{2,1,0:T(8,128)(2,1)}), bf16[16,12,2048]{2,1,0:T(8,128)(2,1)}, u32[]{:S(2)}, u32[]{:S(2)}) async-start(bf16[16,12,2048]{2,1,0:T(8,128)(2,1)} %reshape.148), calls=%async_computation.1 | async-start | bytes 2097152 | tf_op jit(solution)/shard_map/all_to_all | solution.py:106
  109.7 2.1 %reshape.151 = bf16[192,2048]{1,0:T(8,128)(2,1)} reshape(bf16[16,12,2048]{2,1,0:T(8,128)(2,1)} %copy-done.3) | data formatting | bytes 1572864 | tf_op jit(solution)/shard_map/reshape | solution.py:100
  111.8 2.1 %reshape.153 = bf16[192,2048]{1,0:T(8,128)(2,1)} reshape(bf16[16,12,2048]{2,1,0:T(8,128)(2,1)} %all-to-all-done.3) | data formatting | bytes 1572864 | tf_op jit(solution)/shard_map/reshape | solution.py:102
  113.9 2.4 %fusion.3 = f32[192,384]{1,0:T(8,128)S(1)} fusion(bf16[192,2048]{1,0:T(8,128)(2,1)} %reshape.151, bf16[1,1,384,2048]{3,2,1,0:T(8,128)(2,1)} %param.19), kind=kOutput, calls=%fused_computation.10 | convolution fusion | flops 301989888 | bytes 2654208 | tf_op jit(solution)/shard_map/dot_general | solution.py:74
  116.3 1.3 fusion.13
  117.6 3.6 %fusion.11 = f32[192,2048]{1,0:T(8,128)} fusion(bf16[1,1,2048,384]{3,2,1,0:T(8,128)(2,1)S(1)} %copy-done.1, f32[192,384]{1,0:T(8,128)S(1)} %fusion.3, bf16[192,2048]{1,0:T(8,128)(2,1)} %reshape.153, bf16[1,1,2048,384]{3,2,1,0:T(8,128)(2,1)S(1)} %copy-done, f32[192,384]{1,0:T(8,128)} %fusion.13), kind=kOutput, calls=%fused_computation.18 | convolution fusion | flops 604717056 | bytes 6094848 | tf_op jit(solution)/shard_map/dot_general | solution.py:80
  121.2 2.2 %fusion = bf16[192,2048]{1,0:T(8,128)(2,1)S(1)} fusion(f32[192,2048]{1,0:T(8,128)} %fusion.11, bf16[1,1,2048,384]{3,2,1,0:T(8,128)(2,1)S(1)} %copy-done, f32[192,384]{1,0:T(8,128)S(1)} %fusion.3, f32[192,384]{1,0:T(8,128)} %fusion.13), kind=kOutput, calls=%fused_computation.1 | convolution fusion | flops 303218688 | bytes 4521984 | tf_op jit(solution)/shard_map/dot_general | solution.py:81
  123.4 1.2 reshape.154
  124.6 8.0 %all-to-all-done.1 = bf16[16,12,2048]{2,1,0:T(8,128)(2,1)} async-done(((bf16[16,12,2048]{2,1,0:T(8,128)(2,1)}), bf16[16,12,2048]{2,1,0:T(8,128)(2,1)}, u32[]{:S(2)}, u32[]{:S(2)}) %all-to-all-start.1) | async-done | bytes 786464 | tf_op jit(solution)/shard_map/all_to_all | solution.py:106
  132.7 6.8 %all-to-all-start.4 = ((bf16[16,12,2048]{2,1,0:T(8,128)(2,1)}), bf16[16,12,2048]{2,1,0:T(8,128)(2,1)S(1)}, u32[]{:S(2)}, u32[]{:S(2)}) async-start(bf16[16,12,2048]{2,1,0:T(8,128)(2,1)} %reshape.154), calls=%async_computation.4 | async-start | bytes 2097152 | tf_op jit(solution)/shard_map/all_to_all | solution.py:119
  139.5 1.3 reshape.149
  140.8 0.0 copy-done.6
  140.8 1.1 fusion.1
  141.9 1.5 collective-permute-start
  143.4 19.0 %all-to-all-done.4 = bf16[16,12,2048]{2,1,0:T(8,128)(2,1)S(1)} async-done(((bf16[16,12,2048]{2,1,0:T(8,128)(2,1)}), bf16[16,12,2048]{2,1,0:T(8,128)(2,1)S(1)}, u32[]{:S(2)}, u32[]{:S(2)}) %all-to-all-start.4) | async-done | bytes 786464 | tf_op jit(solution)/shard_map/all_to_all | solution.py:119
  162.3 0.2 reshape.155
  162.5 0.4 fusion.2
  162.9 1.6 collective-permute-start.1
  164.5 0.0 collective-permute-done
  164.5 3.9 %collective-permute-done.1 = bf16[1,24,2048]{2,1,0:T(8,128)(2,1)S(1)} collective-permute-done((bf16[1,24,2048]{2,1,0:T(8,128)(2,1)S(1)}, bf16[1,24,2048]{2,1,0:T(8,128)(2,1)S(1)}, u32[]{:S(2)}, u32[]{:S(2)}) %collective-permute-start.1) | collective-permute-done | bytes 98336 | tf_op jit(solution)/shard_map/ppermute | solution.py:11
  168.4 1.5 copy.32
  170.0 0.6 copy.33
  (8 shorter events, 0.0 us)
Async XLA Ops:
  0.6 83.1 %copy-start = (bf16[1,1,2048,384]{3,2,1,0:T(8,128)(2,1)S(1)}, bf16[1,1,2048,384]{3,2,1,0:T(8,128)(2,1)}, u32[]{:S(2)}) copy-start(bf16[1,1,2048,384]{3,2,1,0:T(8,128)(2,1)} %param.18) | copy-start | bytes 4718596
  11.8 8.6 %copy-start.5 = (bf16[1,24,2048]{2,1,0:T(8,128)(2,1)S(1)}, bf16[1,24,2048]{2,1,0:T(8,128)(2,1)}, u32[]{:S(2)}) copy-start(bf16[1,24,2048]{2,1,0:T(8,128)(2,1)} %param.10) | copy-start | bytes 294916
  13.0 30.3 %all-to-all-start.2 = ((bf16[16,12,2048]{2,1,0:T(8,128)(2,1)}), bf16[16,12,2048]{2,1,0:T(8,128)(2,1)S(1)}, u32[]{:S(2)}, u32[]{:S(2)}) async-start(bf16[16,12,2048]{2,1,0:T(8,128)(2,1)} %reshape.150), calls=%async_computation.2 | async-start | bytes 2097152 | tf_op jit(solution)/shard_map/all_to_all | solution.py:117
  20.8 29.3 %copy-start.4 = (f32[24,192]{1,0:T(8,128)S(1)}, f32[24,192]{1,0:T(8,128)}, u32[]{:S(2)}) copy-start(f32[24,192]{1,0:T(8,128)} %get-tuple-element.3) | copy-start | bytes 55300
  43.3 8.1 %copy-start.3 = (bf16[16,12,2048]{2,1,0:T(8,128)(2,1)}, bf16[16,12,2048]{2,1,0:T(8,128)(2,1)S(1)}, u32[]{:S(2)}) copy-start(bf16[16,12,2048]{2,1,0:T(8,128)(2,1)S(1)} %all-to-all-done.2) | copy-start | bytes 2359300
  43.3 29.8 %all-to-all-start = ((bf16[16,12,2048]{2,1,0:T(8,128)(2,1)}), bf16[16,12,2048]{2,1,0:T(8,128)(2,1)}, u32[]{:S(2)}, u32[]{:S(2)}) async-start(bf16[16,12,2048]{2,1,0:T(8,128)(2,1)} %reshape.146), calls=%async_computation | async-start | bytes 2097152 | tf_op jit(solution)/shard_map/all_to_all | solution.py:105
  52.6 29.4 %copy-start.1 = (bf16[1,1,2048,384]{3,2,1,0:T(8,128)(2,1)S(1)}, bf16[1,1,2048,384]{3,2,1,0:T(8,128)(2,1)}, u32[]{:S(2)}) copy-start(bf16[1,1,2048,384]{3,2,1,0:T(8,128)(2,1)} %param.17) | copy-start | bytes 4718596
  73.1 29.8 %all-to-all-start.3 = ((bf16[16,12,2048]{2,1,0:T(8,128)(2,1)}), bf16[16,12,2048]{2,1,0:T(8,128)(2,1)}, u32[]{:S(2)}, u32[]{:S(2)}) async-start(bf16[16,12,2048]{2,1,0:T(8,128)(2,1)} %reshape.152), calls=%async_computation.3 | async-start | bytes 2097152 | tf_op jit(solution)/shard_map/all_to_all | solution.py:116
  102.9 29.8 %all-to-all-start.1 = ((bf16[16,12,2048]{2,1,0:T(8,128)(2,1)}), bf16[16,12,2048]{2,1,0:T(8,128)(2,1)}, u32[]{:S(2)}, u32[]{:S(2)}) async-start(bf16[16,12,2048]{2,1,0:T(8,128)(2,1)} %reshape.148), calls=%async_computation.1 | async-start | bytes 2097152 | tf_op jit(solution)/shard_map/all_to_all | solution.py:106
  113.9 2.4 %copy-start.2 = (bf16[192,2048]{1,0:T(8,128)(2,1)S(1)}, bf16[192,2048]{1,0:T(8,128)(2,1)}, u32[]{:S(2)}) copy-start(bf16[192,2048]{1,0:T(8,128)(2,1)} %reshape.153) | copy-start | bytes 2359300
  124.6 16.2 %copy-start.6 = (f32[24,192]{1,0:T(8,128)S(1)}, f32[24,192]{1,0:T(8,128)}, u32[]{:S(2)}) copy-start(f32[24,192]{1,0:T(8,128)} %get-tuple-element.8) | copy-start | bytes 55300
  132.7 29.7 %all-to-all-start.4 = ((bf16[16,12,2048]{2,1,0:T(8,128)(2,1)}), bf16[16,12,2048]{2,1,0:T(8,128)(2,1)S(1)}, u32[]{:S(2)}, u32[]{:S(2)}) async-start(bf16[16,12,2048]{2,1,0:T(8,128)(2,1)} %reshape.154), calls=%async_computation.4 | async-start | bytes 2097152 | tf_op jit(solution)/shard_map/all_to_all | solution.py:119
  141.9 22.6 %collective-permute-start = (bf16[1,24,2048]{2,1,0:T(8,128)(2,1)}, bf16[1,24,2048]{2,1,0:T(8,128)(2,1)}, u32[]{:S(2)}, u32[]{:S(2)}) collective-permute-start(bf16[1,24,2048]{2,1,0:T(8,128)(2,1)} %fusion.1), channel_id=1, source_target_pairs={{0,16},{16,0},{1,17},{17,1},{2,18},{18,2},{3,19},{19,3},{4,20},{20... | collective-permute-start | bytes 294920 | tf_op jit(solution)/shard_map/ppermute | solution.py:11
  162.9 5.5 %collective-permute-start.1 = (bf16[1,24,2048]{2,1,0:T(8,128)(2,1)S(1)}, bf16[1,24,2048]{2,1,0:T(8,128)(2,1)S(1)}, u32[]{:S(2)}, u32[]{:S(2)}) collective-permute-start(bf16[1,24,2048]{2,1,0:T(8,128)(2,1)S(1)} %fusion.2), channel_id=1, source_target_pairs={{0,16},{16,0},{1,17},{17,1},{2,18},{18,2},{3,19},{19,3},{4,20},{20... | collective-permute-start | bytes 294920 | tf_op jit(solution)/shard_map/ppermute | solution.py:11
where the time goes:
time: 172 us; the launch traced here: 171 us
  waiting for transfers between devices  86.1 us (50%)
  starting transfers between devices  37.8 us (22%)
  local copies, waits for them, and re-layouts  23.3 us (14%)
  matrix products  20 us (12%)
  other arithmetic  2.62 us (2%)
    all_to_all x1, waiting for transfers between devices, body(): lax.all_to_all(grad_rows, 'expert', split_axis=0, concat_axis=0, tiled=True)  21.3 us
    all_to_all x1, waiting for transfers between devices, body(): lax.all_to_all(fwd_rows, 'expert', split_axis=0, concat_axis=0, tiled=True)  20.5 us
    all_to_all x1, waiting for transfers between devices, body(): lax.all_to_all(backward_rows(received[0], received[1]), 'expert', split_a...  19 us
    all_to_all x1, waiting for transfers between devices, body(): lax.all_to_all(bwd_rows, 'expert', split_axis=0, concat_axis=0, tiled=True)  13.4 us
    all_to_all x1, waiting for transfers between devices, body(): lax.all_to_all(expert_forward(received.reshape(-1, width), gate_mat, up_m...  8.05 us
    all_to_all x1, starting transfers between devices, body(): lax.all_to_all(grad_rows, 'expert', split_axis=0, concat_axis=0, tiled=True)  7.41 us
    all_to_all x1, starting transfers between devices, body(): lax.all_to_all(bwd_rows, 'expert', split_axis=0, concat_axis=0, tiled=True)  6.84 us
    all_to_all x1, starting transfers between devices, body(): lax.all_to_all(fwd_rows, 'expert', split_axis=0, concat_axis=0, tiled=True)  6.84 us
  transfers between devices with their start and end apart: 7, of which 6 were waited for; matrix products, arithmetic and copies ran while one was open for 18% of the time, Pallas kernels for 0%

commit v1 on v0

--- a/solution.py
+++ b/solution.py
@@ -1,6 +1,10 @@
+import functools
+
 import jax
 import jax.numpy as jnp
 from jax import lax
+from jax.experimental import pallas as pl
+from jax.experimental.pallas import tpu as pltpu
 from jax.sharding import PartitionSpec as P
 
 TOP = 8
@@ -82,7 +86,7 @@
     return back.astype(jnp.bfloat16)
 
 
-def body(fwd_acts, fwd_ids, fwd_prob, bwd_acts, bwd_ids, bwd_prob, grad_in, w_gate, w_up, w_down):
+def plain_body(fwd_acts, fwd_ids, fwd_prob, bwd_acts, bwd_ids, bwd_prob, grad_in, w_gate, w_up, w_down):
     experts = lax.axis_size("expert")
     tok_count = fwd_acts.shape[1]
     width = fwd_acts.shape[2]
@@ -126,6 +130,353 @@
     return (fwd_out, bwd_out)
 
 
+MESH = pl.DeviceIdType.MESH
+LANES = 128
+NT = (((1,), (1,)), ((), ()))
+BWD, GRAD, FWD = 0, 1, 2
+
+
+def moe_kernel(
+    n,
+    sections,
+    chunks,
+    bwd_ref,
+    grad_ref,
+    fwd_ref,
+    fid_ref,
+    fpr_ref,
+    bid_ref,
+    bpr_ref,
+    wg_ref,
+    wu_ref,
+    wd_ref,
+    fout_ref,
+    bout_ref,
+    gat,
+    prob,
+    xbuf,
+    gbuf,
+    wgate,
+    wup,
+    wdown,
+    part,
+    mid,
+    own,
+    ysend,
+    yrecv,
+    zsend,
+    zrecv,
+    local_sem,
+    wlocal_sem,
+    wsend_sem,
+    wrecv_sem,
+    az_send,
+    az_recv,
+    ay_send,
+    ay_recv,
+    ry_send,
+    ry_recv,
+    rz_send,
+    rz_recv,
+):
+    far = n // 4
+    tok, width = bwd_ref.shape
+    hid = wd_ref.shape[0]
+    rows = 2 * far * tok
+    cw = width // chunks
+    sec = lax.axis_index("segment")
+    me = lax.axis_index("expert")
+    core = lax.rem(me, 2)
+    y = lax.rem(me // 2, 2)
+    z = me // 4
+
+    def place(zz, yy, cc):
+        return (zz * 2 + yy) * 2 + cc
+
+    partner = place(z, y, 1 - core)
+    across = place(z, 1 - y, core)
+    next_sec = lax.rem(sec + 1, sections)
+    prev_sec = lax.rem(sec + sections - 1, sections)
+    peers = [lax.rem(z + d, far) for d in range(1, far)]
+
+    barrier = pltpu.get_barrier_semaphore()
+    greeted = [(sec, partner), (sec, across)] + [(sec, place(p, y, core)) for p in peers]
+    for other in [next_sec] if sections == 2 else [next_sec, prev_sec]:
+        greeted += [(other, place(zz, y, core)) for zz in range(far)]
+    for target in greeted:
+        pl.semaphore_signal(barrier, inc=1, device_id=target, device_id_type=MESH)
+
+    local = []
+    for a, ref in ((BWD, bwd_ref), (GRAD, grad_ref), (FWD, fwd_ref)):
+        local.append(pltpu.make_async_copy(ref, gat.at[a, 0, z], local_sem.at[a]))
+    for cp in local:
+        cp.start()
+    wlocal = [
+        pltpu.make_async_copy(ref, buf.at[0], wlocal_sem.at[k])
+        for k, (ref, buf) in enumerate(((wg_ref, wgate), (wu_ref, wup), (wd_ref, wdown)))
+    ]
+    for cp in wlocal:
+        cp.start()
+    lanes = prob.shape[-1]
+    lane = lax.broadcasted_iota(jnp.int32, (tok, lanes), 1)
+    table = jnp.zeros((tok, lanes), jnp.float32)
+    for k in range(fid_ref.shape[1]):
+        table += jnp.where(fid_ref[:, k : k + 1] == lane, fpr_ref[:, k : k + 1], 0.0)
+        table += jnp.where(bid_ref[:, k : k + 1] + n == lane, bpr_ref[:, k : k + 1], 0.0)
+    prob[0, z] = table
+
+    pl.semaphore_wait(barrier, len(greeted))
+
+    def view(a):
+        return prob if a == 3 else gat.at[a]
+
+    def remote(src, dst, send, recv, device):
+        return pltpu.make_async_remote_copy(
+            src_ref=src,
+            dst_ref=dst,
+            send_sem=send,
+            recv_sem=recv,
+            device_id=device,
+            device_id_type=MESH,
+        )
+
+    def z_copy(a, src, k, p):
+        return remote(
+            src, view(a).at[0, z], az_send.at[a, k], az_recv.at[a, z], (sec, place(p, y, core))
+        )
+
+    def y_copy(a, src, zs):
+        return remote(src, view(a).at[1, zs], ay_send.at[a, zs], ay_recv.at[a, zs], (sec, across))
+
+    started = []
+    for a, ref in ((BWD, bwd_ref), (GRAD, grad_ref), (3, prob.at[0, z]), (FWD, fwd_ref)):
+        for k, p in enumerate(peers):
+            cp = z_copy(a, ref, k, p)
+            cp.start()
+            started.append(cp)
+        cp = y_copy(a, ref, z)
+        cp.start()
+        started.append(cp)
+        if a == BWD:
+            for k, (w, buf) in enumerate(((wg_ref, wgate), (wu_ref, wup), (wd_ref, wdown))):
+                cp = remote(
+                    w, buf.at[1], wsend_sem.at[k], wrecv_sem.at[k], (sec, partner)
+                )
+                cp.start()
+                started.append(cp)
+
+    def forward_rows(a):
+        for d in range(1, far):
+            zs = lax.rem(z + far - d, far)
+            ref = view(a).at[0, zs]
+            remote(ref, ref, az_send.at[a, 0], az_recv.at[a, zs], (sec, across)).wait_recv()
+            cp = y_copy(a, ref, zs)
+            cp.start()
+            started.append(cp)
+
+    def arrive(a):
+        for zs in range(far):
+            ref = view(a).at[1, zs]
+            remote(ref, ref, ay_send.at[a, zs], ay_recv.at[a, zs], (sec, across)).wait_recv()
+
+    def flatten(a, dst):
+        for b in range(far):
+            both = []
+            for q in (2 * b, 2 * b + 1):
+                both.append(gat[a, q // far, q % far].astype(jnp.float32))
+            dst[2 * b * tok : (2 * b + 2) * tok, :] = jnp.concatenate(both, axis=0).astype(
+                jnp.bfloat16
+            )
+
+    def weight_of(base, slot):
+        index = base + (me if slot == 0 else partner)
+        full = prob[...].reshape(rows, lanes)
+        at = lax.broadcasted_iota(jnp.int32, (rows, lanes), 1) == index
+        return jnp.sum(jnp.where(at, full, 0.0), axis=1, keepdims=True)
+
+    def partial_out(r, c, value):
+        half = far * tok
+        own[r, c] = value[:half]
+        for zz in range(far):
+            lo = half + zz * tok
+            ysend[r, c, zz] = value[lo : lo + tok].astype(jnp.bfloat16)
+        cp = remote(
+            ysend.at[r, c], yrecv.at[r, c], ry_send.at[r, c], ry_recv.at[r, c], (sec, across)
+        )
+        cp.start()
+        started.append(cp)
+
+    def second_hop(r, section):
+        for c in range(chunks):
+            remote(
+                ysend.at[r, c], yrecv.at[r, c], ry_send.at[r, c], ry_recv.at[r, c], (sec, across)
+            ).wait_recv()
+            for zz in range(far):
+                total = own[r, c, zz * tok : (zz + 1) * tok] + yrecv[r, c, zz].astype(jnp.float32)
+                zsend[r, c, zz] = total.astype(jnp.bfloat16)
+            for zz in range(far):
+                cp = remote(
+                    zsend.at[r, c, zz],
+                    zrecv.at[r, c, z],
+                    rz_send.at[r, c, zz],
+                    rz_recv.at[r, c, z],
+                    (section, place(zz, y, core)),
+                )
+                cp.start()
+                started.append(cp)
+
+    def finish(r, section, out_ref):
+        for c in range(chunks):
+            total = None
+            for zz in range(far):
+                ref = zrecv.at[r, c, zz]
+                remote(
+                    ref, ref, rz_send.at[r, c, zz], rz_recv.at[r, c, zz], (section, me)
+                ).wait_recv()
+                got = zrecv[r, c, zz].astype(jnp.float32)
+                total = got if total is None else total + got
+            out_ref[:, c * cw : (c + 1) * cw] = total.astype(jnp.bfloat16)
+
+    def mm(a, b):
+        return jnp.dot(a, b, preferred_element_type=jnp.float32)
+
+    def mm_t(a, b):
+        return lax.dot_general(a, b, NT, preferred_element_type=jnp.float32)
+
+    forward_rows(BWD)
+    forward_rows(GRAD)
+    forward_rows(3)
+    local[BWD].wait()
+    arrive(BWD)
+    flatten(BWD, xbuf)
+    for slot in range(2):
+        for k in range(3):
+            if slot == 0:
+                wlocal[k].wait()
+            else:
+                buf = (wgate, wup, wdown)[k].at[1]
+                remote(buf, buf, wsend_sem.at[k], wrecv_sem.at[k], (sec, partner)).wait_recv()
+        part[0] = mm(xbuf[...], wgate[slot])
+        part[1] = mm(xbuf[...], wup[slot])
+        if slot == 0:
+            local[GRAD].wait()
+            arrive(GRAD)
+            arrive(3)
+            flatten(GRAD, gbuf)
+        grad_hidden = mm_t(gbuf[...], wdown[slot]) * weight_of(n, slot)
+        gate_pre = part[0]
+        sigma = jax.nn.sigmoid(gate_pre)
+        mid[2 * slot] = (
+            grad_hidden * part[1] * sigma * (1.0 + gate_pre * (1.0 - sigma))
+        ).astype(jnp.bfloat16)
+        mid[2 * slot + 1] = (grad_hidden * gate_pre * sigma).astype(jnp.bfloat16)
+        if slot == 0:
+            forward_rows(FWD)
+    for c in range(chunks):
+        cols = slice(c * cw, (c + 1) * cw)
+        value = mm_t(mid[0], wgate[0, cols, :])
+        value += mm_t(mid[1], wup[0, cols, :])
+        value += mm_t(mid[2], wgate[1, cols, :])
+        value += mm_t(mid[3], wup[1, cols, :])
+        partial_out(0, c, value)
+
+    local[FWD].wait()
+    arrive(FWD)
+    flatten(FWD, xbuf)
+    for slot in range(2):
+        part[0] = mm(xbuf[...], wgate[slot])
+        up_pre = mm(xbuf[...], wup[slot])
+        gate_pre = part[0]
+        hidden = gate_pre * jax.nn.sigmoid(gate_pre) * up_pre * weight_of(0, slot)
+        mid[slot] = hidden.astype(jnp.bfloat16)
+        if slot == 0:
+            second_hop(0, prev_sec)
+    for c in range(chunks):
+        cols = slice(c * cw, (c + 1) * cw)
+        value = mm(mid[0], wdown[0, :, cols])
+        value += mm(mid[1], wdown[1, :, cols])
+        partial_out(1, c, value)
+    second_hop(1, next_sec)
+    finish(0, prev_sec, bout_ref)
+    finish(1, next_sec, fout_ref)
+    for cp in started:
+        cp.wait_send()
+
+
+def fused_body(n, sections, chunks, *args):
+    fwd_acts, fwd_ids, fwd_prob, bwd_acts, bwd_ids, bwd_prob, grad_in, w_gate, w_up, w_down = args
+    tok, width = fwd_acts.shape[1:]
+    hid = w_down.shape[2]
+    far = n // 4
+    rows = 2 * far * tok
+    cw = width // chunks
+    lanes = -(-2 * n // LANES) * LANES
+    bf, f32 = jnp.bfloat16, jnp.float32
+    dma = pltpu.SemaphoreType.DMA
+    fwd_out, bwd_out = pl.pallas_call(
+        functools.partial(moe_kernel, n, sections, chunks),
+        out_shape=[jax.ShapeDtypeStruct((tok, width), bf)] * 2,
+        in_specs=[pl.BlockSpec(memory_space=pl.ANY)] * 3
+        + [pl.BlockSpec(memory_space=pltpu.VMEM)] * 4
+        + [pl.BlockSpec(memory_space=pl.ANY)] * 3,
+        out_specs=[pl.BlockSpec(memory_space=pltpu.VMEM)] * 2,
+        scratch_shapes=[
+            pltpu.VMEM((3, 2, far, tok, width), bf),
+            pltpu.VMEM((2, far, tok, lanes), f32),
+            pltpu.VMEM((rows, width), bf),
+            pltpu.VMEM((rows, width), bf),
+            pltpu.VMEM((2, width, hid), bf),
+            pltpu.VMEM((2, width, hid), bf),
+            pltpu.VMEM((2, hid, width), bf),
+            pltpu.VMEM((2, rows, hid), f32),
+            pltpu.VMEM((4, rows, hid), bf),
+            pltpu.VMEM((2, chunks, far * tok, cw), f32),
+            pltpu.VMEM((2, chunks, far, tok, cw), bf),
+            pltpu.VMEM((2, chunks, far, tok, cw), bf),
+            pltpu.VMEM((2, chunks, far, tok, cw), bf),
+            pltpu.VMEM((2, chunks, far, tok, cw), bf),
+            dma((3,)),
+            dma((3,)),
+            dma((3,)),
+            dma((3,)),
+            dma((4, far)),
+            dma((4, far)),
+            dma((4, far)),
+            dma((4, far)),
+            dma((2, chunks)),
+            dma((2, chunks)),
+            dma((2, chunks, far)),
+            dma((2, chunks, far)),
+        ],
+        compiler_params=pltpu.CompilerParams(
+            collective_id=0, has_side_effects=True, vmem_limit_bytes=60 * 1024 * 1024
+        ),
+    )(
+        bwd_acts[0],
+        grad_in[0],
+        fwd_acts[0],
+        fwd_ids[0],
+        fwd_prob[0],
+        bwd_ids[0],
+        bwd_prob[0],
+        w_gate[0, 0],
+        w_up[0, 0],
+        w_down[0, 0],
+    )
+    return fwd_out[None], bwd_out[None]
+
+
+def body(*args):
+    n = lax.axis_size("expert")
+    sections = lax.axis_size("segment")
+    tok, width = args[0].shape[1:]
+    gathered = n * tok * width * 2
+    fits = n % 4 == 0 and n >= 8 and sections > 1 and tok % 8 == 0 and width % 512 == 0
+    if not fits or gathered > 4 * 1024 * 1024:
+        return plain_body(*args)
+    return fused_body(n, sections, width // 512, *args)
+
+
 def solution(mesh):
     return jax.shard_map(
         body,

time: 172 us -> 76.3 us (0.44)
  waiting for transfers between devices: 86.1 us -> 0 us
  Pallas kernels: 0 us -> 66 us
  starting transfers between devices: 37.8 us -> 0 us
  matrix products: 20 us -> 0 us
  local copies, waits for them, and re-layouts: 23.3 us -> 8.5 us
  other arithmetic: 2.62 us -> 0 us
    all_to_all x5 -> x0, waiting for transfers between devices: 82.2 us -> none  [the longest x1 21.3 us: body(): lax.all_to_all(grad_rows, 'expert', split_axis=0, concat_axis=0, tiled=True)]
    pallas_call x0 -> x1, Pallas kernels: none -> 66 us  [fused_body(): pl.pallas_call(functools.partial(moe_kernel, n, sections, chunks), out_sh...]
    all_to_all x5 -> x0, starting transfers between devices: 34.7 us -> none  [the longest x1 7.41 us: body(): lax.all_to_all(grad_rows, 'expert', split_axis=0, concat_axis=0, tiled=True)]
    dot_general x13 -> x0, matrix products: 20 us -> none  [the longest x1 3.65 us: expert_forward(): jnp.dot(hidden, down_mat, preferred_element_type=jnp.float32)]
    reshape x10 -> x0, local copies, waits for them, and re-layouts: 14.6 us -> none  [the longest x1 2.12 us: body(): expert_forward(received.reshape(-1, width), gate_mat, up_mat, down_mat)]
    unnamed x18 -> x6, local copies, waits for them, and re-layouts: 3.86 us -> 8.5 us
    mul x4 -> x0, local copies, waits for them, and re-layouts: 4.24 us -> none  [the longest x2 2.72 us: routing(): weigh_mat = jnp.sum(placed * gate_prob[:, :, None], axis=1)]
    ppermute x2 -> x0, waiting for transfers between devices: 3.91 us -> none  [shifted(): lax.ppermute(array, axis, [(i, (i + by) % count) for i in range(count)])]
  transfers between devices with their start and end apart: 7 -> 0, of which waited for: 6 -> 0; matrix products, arithmetic and copies ran while one was open for 18% -> 0% of each run, Pallas kernels for 0% -> 0%
where the time goes in v1:
time: 76.3 us; the launch traced here: 75.1 us
  Pallas kernels  66 us (87%)
  local copies, waits for them, and re-layouts  8.5 us (11%)
    pallas_call x1, Pallas kernels, fused_body(): pl.pallas_call(functools.partial(moe_kernel, n, sections, chunks), out_sh...  66 us
    unnamed x6, local copies, waits for them, and re-layouts  8.5 us

profile of v1, /device:TPU:0, one launch (start us, length us, event | category | flops | bytes accessed | tf_op | source)
XLA Modules:
  0.0 75.1 jit_solution(2333544320301670527)
XLA Ops:
  0.6 1.4 %copy.12 = s32[1,24,8]{2,1,0:T(8,128)} copy(s32[1,24,8]{1,2,0:T(8,128)} %param.11) | data formatting | bytes 1536 | tf_op args[1]
  2.0 1.4 %copy.13 = f32[1,24,8]{2,1,0:T(8,128)} copy(f32[1,24,8]{1,2,0:T(8,128)} %param.12) | data formatting | bytes 1536 | tf_op args[2]
  3.3 1.4 %copy.14 = s32[1,24,8]{2,1,0:T(8,128)} copy(s32[1,24,8]{1,2,0:T(8,128)} %param.14) | data formatting | bytes 1536 | tf_op args[4]
  4.7 1.4 %copy.15 = f32[1,24,8]{2,1,0:T(8,128)} copy(f32[1,24,8]{1,2,0:T(8,128)} %param.15) | data formatting | bytes 1536 | tf_op args[5]
  6.1 66.0 %shard_map.113 = (bf16[24,2048]{1,0:T(8,128)(2,1)}, bf16[24,2048]{1,0:T(8,128)(2,1)}) custom-call(bf16[24,2048]{1,0:T(8,128)(2,1)} %bitcast.17, bf16[24,2048]{1,0:T(8,128)(2,1)} %bitcast.18, bf16[24,2048]{1,0:T(8,128)(2,1)} %bitcast.19, s32[24,8]{1,0:T(8,128)} %bitcast.20, f32[24,8]{1,0:T(8,128)} %bitcast.21, s32[24,8]{1,0:T(8,128)} %bitcast.22, ...), custom_call_target="tpu_custom_call" | custom-call | tf_op jit(solution)/shard_map/pallas_call | solution.py:416
  72.0 1.5 %copy.18 = bf16[1,24,2048]{2,1,0:T(8,128)(2,1)} copy(bf16[1,24,2048]{2,1,0:T(8,128)(2,1)} %bitcast.16) | data formatting | bytes 196608
  73.6 1.5 %copy.19 = bf16[1,24,2048]{2,1,0:T(8,128)(2,1)} copy(bf16[1,24,2048]{2,1,0:T(8,128)(2,1)} %bitcast.15) | data formatting | bytes 196608

commit v2 on v1

--- a/solution.py
+++ b/solution.py
@@ -218,12 +218,12 @@
     for cp in wlocal:
         cp.start()
     lanes = prob.shape[-1]
-    lane = lax.broadcasted_iota(jnp.int32, (tok, lanes), 1)
-    table = jnp.zeros((tok, lanes), jnp.float32)
-    for k in range(fid_ref.shape[1]):
-        table += jnp.where(fid_ref[:, k : k + 1] == lane, fpr_ref[:, k : k + 1], 0.0)
-        table += jnp.where(bid_ref[:, k : k + 1] + n == lane, bpr_ref[:, k : k + 1], 0.0)
-    prob[0, z] = table
+    line = lax.broadcasted_iota(jnp.int32, (lanes, tok), 0)
+    table = jnp.zeros((lanes, tok), jnp.float32)
+    for k in range(fid_ref.shape[0]):
+        table += jnp.where(fid_ref[k : k + 1, :] == line, fpr_ref[k : k + 1, :], 0.0)
+        table += jnp.where(bid_ref[k : k + 1, :] + n == line, bpr_ref[k : k + 1, :], 0.0)
+    prob[0, z] = table.T
 
     pl.semaphore_wait(barrier, len(greeted))
 
@@ -240,39 +240,59 @@
             device_id_type=MESH,
         )
 
-    def z_copy(a, src, k, p):
+    def z_copy(a, src, zs, way):
         return remote(
-            src, view(a).at[0, z], az_send.at[a, k], az_recv.at[a, z], (sec, place(p, y, core))
+            src,
+            view(a).at[0, zs],
+            az_send.at[a, way, zs],
+            az_recv.at[a, zs],
+            (sec, place(z + (1 - 2 * way), y, core)),
         )
 
     def y_copy(a, src, zs):
         return remote(src, view(a).at[1, zs], ay_send.at[a, zs], ay_recv.at[a, zs], (sec, across))
 
     started = []
-    for a, ref in ((BWD, bwd_ref), (GRAD, grad_ref), (3, prob.at[0, z]), (FWD, fwd_ref)):
-        for k, p in enumerate(peers):
-            cp = z_copy(a, ref, k, p)
-            cp.start()
-            started.append(cp)
+    guarded = []
+
+    def onward(a, src, zs, valid):
+        for way, there in valid:
+            cp = z_copy(a, src, zs, way)
+            pl.when(there)(cp.start)
+            guarded.append((there, cp))
+
+    def send_own(a, ref):
+        onward(a, ref, z, ((0, z + 1 < far), (1, z > 0)))
         cp = y_copy(a, ref, z)
         cp.start()
         started.append(cp)
-        if a == BWD:
-            for k, (w, buf) in enumerate(((wg_ref, wgate), (wu_ref, wup), (wd_ref, wdown))):
-                cp = remote(
-                    w, buf.at[1], wsend_sem.at[k], wrecv_sem.at[k], (sec, partner)
-                )
+
+    def relay(a, hops):
+        for way in range(2):
+            step = 1 - 2 * way
+            zs = z - step * (hops + 1)
+            here = jnp.logical_and(zs >= 0, zs < far)
+            further = jnp.logical_and(here, z + 1 < far if way == 0 else z > 0)
+            ref = view(a).at[0, zs]
+            cp = y_copy(a, ref, zs)
+            on = z_copy(a, ref, zs, way)
+
+            @pl.when(here)
+            def _():
+                on.wait_recv()
+                pl.when(further)(on.start)
                 cp.start()
-                started.append(cp)
-
-    def forward_rows(a):
-        for d in range(1, far):
-            zs = lax.rem(z + far - d, far)
-            ref = view(a).at[0, zs]
-            remote(ref, ref, az_send.at[a, 0], az_recv.at[a, zs], (sec, across)).wait_recv()
-            cp = y_copy(a, ref, zs)
-            cp.start()
-            started.append(cp)
+
+            guarded.append((here, cp))
+            guarded.append((further, on))
+
+    send_own(BWD, bwd_ref)
+    send_own(GRAD, grad_ref)
+    send_own(3, prob.at[0, z])
+    for k, (w, buf) in enumerate(((wg_ref, wgate), (wu_ref, wup), (wd_ref, wdown))):
+        cp = remote(w, buf.at[1], wsend_sem.at[k], wrecv_sem.at[k], (sec, partner))
+        cp.start()
+        started.append(cp)
 
     def arrive(a):
         for zs in range(far):
@@ -343,9 +363,13 @@
     def mm_t(a, b):
         return lax.dot_general(a, b, NT, preferred_element_type=jnp.float32)
 
-    forward_rows(BWD)
-    forward_rows(GRAD)
-    forward_rows(3)
+    for hops in range(far - 1):
+        if hops == far - 2:
+            send_own(FWD, fwd_ref)
+        for a in (BWD, GRAD, 3):
+            relay(a, hops)
+        if hops == far - 2:
+            relay(FWD, 0)
     local[BWD].wait()
     arrive(BWD)
     flatten(BWD, xbuf)
@@ -371,7 +395,8 @@
         ).astype(jnp.bfloat16)
         mid[2 * slot + 1] = (grad_hidden * gate_pre * sigma).astype(jnp.bfloat16)
         if slot == 0:
-            forward_rows(FWD)
+            for hops in range(1, far - 1):
+                relay(FWD, hops)
     for c in range(chunks):
         cols = slice(c * cw, (c + 1) * cw)
         value = mm_t(mid[0], wgate[0, cols, :])
@@ -401,6 +426,8 @@
     finish(1, next_sec, fout_ref)
     for cp in started:
         cp.wait_send()
+    for there, cp in guarded:
+        pl.when(there)(cp.wait_send)
 
 
 def fused_body(n, sections, chunks, *args):
@@ -439,7 +466,7 @@
             dma((3,)),
             dma((3,)),
             dma((3,)),
-            dma((4, far)),
+            dma((4, 2, far)),
             dma((4, far)),
             dma((4, far)),
             dma((4, far)),
@@ -455,10 +482,10 @@
         bwd_acts[0],
         grad_in[0],
         fwd_acts[0],
-        fwd_ids[0],
-        fwd_prob[0],
-        bwd_ids[0],
-        bwd_prob[0],
+        fwd_ids[0].T,
+        fwd_prob[0].T,
+        bwd_ids[0].T,
+        bwd_prob[0].T,
         w_gate[0, 0],
         w_up[0, 0],
         w_down[0, 0],

time: 76.3 us -> 62.9 us (0.82); the launches traced: 75.1 us -> 62.7 us
  Pallas kernels: 66 us -> 59 us
  local copies, waits for them, and re-layouts: 8.5 us -> 3.08 us
    pallas_call x1, Pallas kernels: 66 us -> 59 us  [fused_body(): pl.pallas_call(functools.partial(moe_kernel, n, sections, chunks), out_sh...]
    unnamed x6 -> x2, local copies, waits for them, and re-layouts: 8.5 us -> 3.08 us
where the time goes in v2:
time: 62.9 us; the launch traced here: 62.7 us
  Pallas kernels  59 us (94%)
  local copies, waits for them, and re-layouts  3.08 us (5%)
  between operations  0.64 us (1%)
    pallas_call x1, Pallas kernels, fused_body(): pl.pallas_call(functools.partial(moe_kernel, n, sections, chunks), out_sh...  59 us
    unnamed x2, local copies, waits for them, and re-layouts  3.08 us

profile of v2, /device:TPU:0, one launch (start us, length us, event | category | flops | bytes accessed | tf_op | source)
XLA Modules:
  0.0 62.7 jit_solution(16121162889193555860)
XLA Ops:
  0.6 59.0 %shard_map.113 = (bf16[24,2048]{1,0:T(8,128)(2,1)}, bf16[24,2048]{1,0:T(8,128)(2,1)}) custom-call(bf16[24,2048]{1,0:T(8,128)(2,1)} %bitcast.25, bf16[24,2048]{1,0:T(8,128)(2,1)} %bitcast.26, bf16[24,2048]{1,0:T(8,128)(2,1)} %bitcast.27, s32[8,24]{1,0:T(8,128)} %bitcast.28, f32[8,24]{1,0:T(8,128)} %bitcast.29, s32[8,24]{1,0:T(8,128)} %bitcast.30, ...), custom_call_target="tpu_custom_call" | custom-call | tf_op jit(solution)/shard_map/pallas_call | solution.py:443
  59.6 1.5 %copy.14 = bf16[1,24,2048]{2,1,0:T(8,128)(2,1)} copy(bf16[1,24,2048]{2,1,0:T(8,128)(2,1)} %bitcast.24) | data formatting | bytes 196608
  61.2 1.5 %copy.15 = bf16[1,24,2048]{2,1,0:T(8,128)(2,1)} copy(bf16[1,24,2048]{2,1,0:T(8,128)(2,1)} %bitcast.23) | data formatting | bytes 196608

commit v3 on v2

--- a/solution.py
+++ b/solution.py
@@ -174,6 +174,9 @@
     az_recv,
     ay_send,
     ay_recv,
+    bz_send,
+    bz_recv,
+    by_sem,
     ry_send,
     ry_recv,
     rz_send,
@@ -227,8 +230,17 @@
 
     pl.semaphore_wait(barrier, len(greeted))
 
-    def view(a):
-        return prob if a == 3 else gat.at[a]
+    cut = width // 2
+
+    def block(a, row, zs):
+        if a == 3:
+            return prob.at[row, zs]
+        if a == FWD:
+            return gat.at[a, row, zs, :, pl.ds(0, cut)]
+        return gat.at[a, row, zs]
+
+    def late(row, zs):
+        return gat.at[FWD, row, zs, :, pl.ds(cut, width - cut)]
 
     def remote(src, dst, send, recv, device):
         return pltpu.make_async_remote_copy(
@@ -243,14 +255,14 @@
     def z_copy(a, src, zs, way):
         return remote(
             src,
-            view(a).at[0, zs],
+            block(a, 0, zs),
             az_send.at[a, way, zs],
             az_recv.at[a, zs],
             (sec, place(z + (1 - 2 * way), y, core)),
         )
 
     def y_copy(a, src, zs):
-        return remote(src, view(a).at[1, zs], ay_send.at[a, zs], ay_recv.at[a, zs], (sec, across))
+        return remote(src, block(a, 1, zs), ay_send.at[a, zs], ay_recv.at[a, zs], (sec, across))
 
     started = []
     guarded = []
@@ -273,7 +285,7 @@
             zs = z - step * (hops + 1)
             here = jnp.logical_and(zs >= 0, zs < far)
             further = jnp.logical_and(here, z + 1 < far if way == 0 else z > 0)
-            ref = view(a).at[0, zs]
+            ref = block(a, 0, zs)
             cp = y_copy(a, ref, zs)
             on = z_copy(a, ref, zs, way)
 
@@ -286,8 +298,41 @@
             guarded.append((here, cp))
             guarded.append((further, on))
 
+    def late_copy(row, src, zs, way):
+        return remote(
+            src,
+            late(row, zs),
+            bz_send.at[row, way, zs],
+            bz_recv.at[row, zs],
+            (sec, place(z + (1 - 2 * way), y, core)),
+        )
+
+    def late_send(row, src):
+        for way, there in ((0, z + 1 < far), (1, z > 0)):
+            cp = late_copy(row, src, z, way)
+            pl.when(there)(cp.start)
+            guarded.append((there, cp))
+
+    def late_relay(row, hops):
+        for way in range(2):
+            zs = z - (1 - 2 * way) * (hops + 1)
+            here = jnp.logical_and(zs >= 0, zs < far)
+            further = jnp.logical_and(here, z + 1 < far if way == 0 else z > 0)
+            on = late_copy(row, late(row, zs), zs, way)
+
+            @pl.when(here)
+            def _():
+                on.wait_recv()
+                pl.when(further)(on.start)
+
+            guarded.append((further, on))
+
+    fwd_late = fwd_ref.at[:, pl.ds(cut, width - cut)]
+    late_across = remote(fwd_late, late(1, z), by_sem.at[0], by_sem.at[1], (sec, across))
     send_own(BWD, bwd_ref)
     send_own(GRAD, grad_ref)
+    late_across.start()
+    started.append(late_across)
     send_own(3, prob.at[0, z])
     for k, (w, buf) in enumerate(((wg_ref, wgate), (wu_ref, wup), (wd_ref, wdown))):
         cp = remote(w, buf.at[1], wsend_sem.at[k], wrecv_sem.at[k], (sec, partner))
@@ -296,7 +341,7 @@
 
     def arrive(a):
         for zs in range(far):
-            ref = view(a).at[1, zs]
+            ref = block(a, 1, zs)
             remote(ref, ref, ay_send.at[a, zs], ay_recv.at[a, zs], (sec, across)).wait_recv()
 
     def flatten(a, dst):
@@ -326,8 +371,8 @@
         cp.start()
         started.append(cp)
 
-    def second_hop(r, section):
-        for c in range(chunks):
+    def second_hop(r, section, which):
+        for c in which:
             remote(
                 ysend.at[r, c], yrecv.at[r, c], ry_send.at[r, c], ry_recv.at[r, c], (sec, across)
             ).wait_recv()
@@ -365,11 +410,16 @@
 
     for hops in range(far - 1):
         if hops == far - 2:
-            send_own(FWD, fwd_ref)
+            send_own(FWD, fwd_ref.at[:, pl.ds(0, cut)])
+            late_send(0, fwd_late)
+            late_across.wait_recv()
+            late_send(1, late(1, z))
         for a in (BWD, GRAD, 3):
             relay(a, hops)
         if hops == far - 2:
             relay(FWD, 0)
+            late_relay(0, 0)
+            late_relay(1, 0)
     local[BWD].wait()
     arrive(BWD)
     flatten(BWD, xbuf)
@@ -394,9 +444,10 @@
             grad_hidden * part[1] * sigma * (1.0 + gate_pre * (1.0 - sigma))
         ).astype(jnp.bfloat16)
         mid[2 * slot + 1] = (grad_hidden * gate_pre * sigma).astype(jnp.bfloat16)
-        if slot == 0:
-            for hops in range(1, far - 1):
-                relay(FWD, hops)
+        for hops in range(1, far - 2) if slot == 0 else range(max(1, far - 2), far - 1):
+            relay(FWD, hops)
+            late_relay(0, hops)
+            late_relay(1, hops)
     for c in range(chunks):
         cols = slice(c * cw, (c + 1) * cw)
         value = mm_t(mid[0], wgate[0, cols, :])
@@ -414,14 +465,13 @@
         gate_pre = part[0]
         hidden = gate_pre * jax.nn.sigmoid(gate_pre) * up_pre * weight_of(0, slot)
         mid[slot] = hidden.astype(jnp.bfloat16)
-        if slot == 0:
-            second_hop(0, prev_sec)
     for c in range(chunks):
         cols = slice(c * cw, (c + 1) * cw)
         value = mm(mid[0], wdown[0, :, cols])
         value += mm(mid[1], wdown[1, :, cols])
         partial_out(1, c, value)
-    second_hop(1, next_sec)
+        second_hop(0, prev_sec, [c])
+    second_hop(1, next_sec, range(chunks))
     finish(0, prev_sec, bout_ref)
     finish(1, next_sec, fout_ref)
     for cp in started:
@@ -470,6 +520,9 @@
             dma((4, far)),
             dma((4, far)),
             dma((4, far)),
+            dma((2, 2, far)),
+            dma((2, far)),
+            dma((2,)),
             dma((2, chunks)),
             dma((2, chunks)),
             dma((2, chunks, far)),

time: 62.9 us -> 60.1 us (0.955)
  Pallas kernels: 59 us -> 56.2 us
    pallas_call x1, Pallas kernels: 59 us -> 56.2 us  [fused_body(): pl.pallas_call(functools.partial(moe_kernel, n, sections, chunks), out_sh...]
where the time goes in v3:
time: 60.1 us; the launch traced here: 59.9 us
  Pallas kernels  56.2 us (94%)
  local copies, waits for them, and re-layouts  3.08 us (5%)
  between operations  0.64 us (1%)
    pallas_call x1, Pallas kernels, fused_body(): pl.pallas_call(functools.partial(moe_kernel, n, sections, chunks), out_sh...  56.2 us
    unnamed x2, local copies, waits for them, and re-layouts  3.08 us

profile of v3, /device:TPU:0, one launch (start us, length us, event | category | flops | bytes accessed | tf_op | source)
XLA Modules:
  0.0 59.9 jit_solution(8933076937554672997)
XLA Ops:
  0.6 56.2 %shard_map.113 = (bf16[24,2048]{1,0:T(8,128)(2,1)}, bf16[24,2048]{1,0:T(8,128)(2,1)}) custom-call(bf16[24,2048]{1,0:T(8,128)(2,1)} %bitcast.25, bf16[24,2048]{1,0:T(8,128)(2,1)} %bitcast.26, bf16[24,2048]{1,0:T(8,128)(2,1)} %bitcast.27, s32[8,24]{1,0:T(8,128)} %bitcast.28, f32[8,24]{1,0:T(8,128)} %bitcast.29, s32[8,24]{1,0:T(8,128)} %bitcast.30, ...), custom_call_target="tpu_custom_call" | custom-call | tf_op jit(solution)/shard_map/pallas_call | solution.py:493
  56.8 1.5 %copy.14 = bf16[1,24,2048]{2,1,0:T(8,128)(2,1)} copy(bf16[1,24,2048]{2,1,0:T(8,128)(2,1)} %bitcast.24) | data formatting | bytes 196608
  58.3 1.5 %copy.15 = bf16[1,24,2048]{2,1,0:T(8,128)(2,1)} copy(bf16[1,24,2048]{2,1,0:T(8,128)(2,1)} %bitcast.23) | data formatting | bytes 196608
